TPU v7x, 512 devices: a whole 4x8x8 slice. The times are simulated.
512 devices in a mesh: fix: 64 (over z, x, core), subj: 8 (over y).
Axes of the slice: x: 4, y: 8, z: 8, core: 2. Of those that a mesh axis runs over, the one named last changes fastest.
Arguments:
- fixels: float32 [65536, 1024], P('fix', 'subj'), may hold values from -6 to 6
- conn_tiles: float32 [512, 4, 128, 128], P('fix'), may hold values from -0.25 to 0.25
- columns: int32 [512, 4], P('fix'), may hold values from 0 to 511, as said below
- nuisance: float32 [4, 1024], P(None, 'subj'), may hold values from -5 to 5
- nuisance_pinv: float32 [4, 1024], P(None, 'subj'), may hold values from -0.1875 to 0.1875
- contrast: float32 [4, 1024], replicated, may hold values from -0.1875 to 0.1875
- perm_table: int32 [128, 1024], P(None, 'subj'), may hold values from 0 to 1023, each once within a row
Outputs:
- projections: float32 [512, 65536], P('subj', 'fix')
Inputs may be any that keep to these rules, and one draw needn't show every extreme that they name: `columns`: device j of fix holds blocks j * 8 to (j + 1) * 8 - 1. The 32 entries of one device's rows name blocks of any one device at most 1 times, and in every draw some device's blocks are named exactly 1 times by the rows of every device. `perm_table`: each row is a permutation of the 1024 subjects.
All inputs are finite; a program needn't handle non-finite values.
Results may differ from a plain program's by a relative error of at most 0.000071.
Values sent between devices are 32-bit elements; how exact they have to be, the bound alone decides.
A program may use at most 64 MiB of HBM per device.

v0:
```python
import jax
import jax.numpy as jnp
from jax import lax
from jax.sharding import PartitionSpec as P


def design_rows(contrast, perm_table):
    picked = jnp.take(contrast, perm_table, axis=1)
    return jnp.transpose(picked, (1, 0, 2)).reshape(-1, perm_table.shape[1])


def per_device(fixels, conn_tiles, columns, nuisance, nuisance_pinv, contrast, perm_table):
    fix_count = lax.axis_size("fix")
    block_count, per_row = columns.shape
    block_size = conn_tiles.shape[2]
    subj_count = fixels.shape[1]
    tile_total = block_count * per_row
    wanted = columns.reshape(tile_total)
    owners = wanted // block_count
    local_index = wanted % block_count
    capacity = (tile_total + fix_count - 1) // fix_count
    positions = jnp.arange(tile_total)
    earlier = positions[:, None] > positions[None, :]
    same_owner = owners[:, None] == owners[None, :]
    ranks = jnp.sum(jnp.logical_and(same_owner, earlier), axis=1)
    slots = owners * capacity + ranks
    request = jnp.zeros((fix_count * capacity,), jnp.int32).at[slots].set(local_index)
    asked = lax.all_to_all(
        request.reshape(fix_count, capacity), "fix", split_axis=0, concat_axis=0, tiled=True
    ).reshape(-1)
    design = design_rows(contrast, perm_table)
    own_blocks = fixels.reshape(block_count, block_size, subj_count)
    outgoing = jnp.take(own_blocks, asked, axis=0).reshape(
        fix_count, capacity, block_size, subj_count
    )
    arrived = lax.all_to_all(outgoing, "fix", split_axis=0, concat_axis=0, tiled=True).reshape(
        fix_count * capacity, block_size, subj_count
    )
    needed = jnp.take(arrived, slots, axis=0).reshape(block_count, per_row, block_size, subj_count)
    smoothed = jnp.einsum(
        "bkij,bkjs->bis", conn_tiles, needed, precision=lax.Precision.HIGHEST
    ).reshape(block_count * block_size, subj_count)
    fitted_part = jnp.einsum("ns,fs->nf", nuisance_pinv, smoothed, precision=lax.Precision.HIGHEST)
    fitted = lax.psum(fitted_part, "subj")
    residual = smoothed - jnp.einsum("nf,ns->fs", fitted, nuisance, precision=lax.Precision.HIGHEST)
    partial_value = jnp.einsum("cs,fs->cf", design, residual, precision=lax.Precision.HIGHEST)
    return lax.psum_scatter(partial_value, "subj", scatter_dimension=0, tiled=True)


def solution(mesh):
    placed = (
        P("fix", "subj"),
        P("fix", None, None, None),
        P("fix", None),
        P(None, "subj"),
        P(None, "subj"),
        P(),
        P(None, "subj"),
    )
    return jax.shard_map(
        per_device, mesh=mesh, in_specs=placed, out_specs=P("subj", "fix"), check_vma=False
    )
```

profile of v0, /device:TPU:6, one launch (start us, length us, event | category | flops | bytes accessed | tf_op | source)
XLA Modules:
  0.0 232.2 jit_solution(1409098919103364654)
XLA Ops:
  6.5 0.0 copy-start
  6.5 0.9 copy.43
  7.4 0.1 reshape.202
  7.5 0.1 reshape.203
  7.6 0.2 convert_reduce_fusion
  7.8 0.7 scatter_custom_fusion
  8.5 0.1 copy.49
  8.6 21.5 %all_to_all.20 = s32[64,1,1]{2,1,0:T(1,128)S(1)} all-to-all(s32[64,1,1]{2,1,0:T(1,128)S(1)} %copy.49), channel_id=1, replica_groups=mesh['fix'=64,'subj'=8] {'fix'}, dimensions={0} | all-to-all | bytes 512 | tf_op jit(solution)/shard_map/all_to_all | solution.py:28
  30.1 1.2 reduce
  31.4 3.8 %gather_fusion.1 = f32[64,128,128]{2,1,0:T(8,128)} fusion(f32[8,128,128]{2,1,0:T(8,128)} %bitcast.37, s32[1024]{0:T(1024)S(1)} %pad_clamp_fusion.1), kind=kCustom, calls=%fused_computation.1 | custom fusion | bytes 8388864 | tf_op jit(solution)/shard_map/jit(_take)/gather | solution.py:33
  35.2 4.5 %bitcast_select_fusion = f32[64,1,128,128]{3,2,1,0:T(8,128)} fusion(f32[64,128,128]{2,1,0:T(8,128)} %gather_fusion.1, pred[64]{0:T(512)(128)(4,1)S(1)} %compare_and_fusion.2), kind=kLoop, calls=%fused_computation.4 | loop fusion | flops 1048576 | bytes 8388672 | tf_op jit(solution)/shard_map/jit(_take)/select_n | solution.py:33
  39.7 7.4 %all-to-all-start.1 = ((f32[64,1,128,128]{3,2,1,0:T(8,128)}), f32[64,1,128,128]{3,2,1,0:T(8,128)}, u32[]{:S(2)}, u32[]{:S(2)}) async-start(f32[64,1,128,128]{3,2,1,0:T(8,128)} %bitcast_select_fusion), calls=%async_computation.1 | async-start | bytes 8388608 | tf_op jit(solution)/shard_map/all_to_all | solution.py:36
  47.1 0.0 reduce-scatter.2.cloned.1.call-start
  47.1 0.1 reduce_sum.14
  47.2 0.0 copy-done.2
  47.2 0.2 copy.41
  47.4 0.0 copy-done.1
  47.5 54.4 %gather_fusion = f32[16384,4]{1,0:T(8,128)} fusion(f32[4,1024]{0,1:T(8,128)S(1)} %copy.41, s32[16384]{0:T(1024)S(1)} %bitcast_clamp_fusion), kind=kCustom, calls=%fused_computation | custom fusion | bytes 589824 | tf_op jit(solution)/shard_map/jit(_take)/gather | solution.py:8
  101.9 5.5 %copy.42 = f32[128,128,4]{1,2,0:T(4,128)S(1)} copy(f32[128,128,4]{2,1,0:T(8,128)} %bitcast.38) | data formatting | bytes 524288 | tf_op jit(solution)/shard_map/jit(_take)/gather | solution.py:8
  107.4 0.1 broadcast_select_fusion
  107.5 35.7 %all-to-all-done.1 = f32[64,1,128,128]{3,2,1,0:T(8,128)} async-done(((f32[64,1,128,128]{3,2,1,0:T(8,128)}), f32[64,1,128,128]{3,2,1,0:T(8,128)}, u32[]{:S(2)}, u32[]{:S(2)}) %all-to-all-start.1) | async-done | bytes 4194336 | tf_op jit(solution)/shard_map/all_to_all | solution.py:36
  143.3 4.2 %gather_fusion.2 = f32[32,128,128]{2,1,0:T(8,128)} fusion(f32[64,128,128]{2,1,0:T(8,128)} %bitcast.10, s32[1024]{0:T(1024)S(1)} %pad_clamp_fusion), kind=kCustom, calls=%fused_computation.2 | custom fusion | bytes 4194432 | tf_op jit(solution)/shard_map/jit(_take)/gather | solution.py:39
  147.5 0.0 copy-done
  147.5 4.1 %fusion = f32[8,128,128,1]{1,2,3,0:T(8,128)S(1)} fusion(f32[8,4,128,128]{3,2,1,0:T(8,128)S(1)} %copy-done, f32[8,4,128,128]{3,2,1,0:T(8,128)} %bitcast.39, pred[8,4]{1,0:T(8,128)(4,1)S(1)} %compare_and_fusion.1), kind=kOutput, calls=%fused_computation.5 | convolution fusion | flops 805830656 | bytes 4718624 | tf_op jit(solution)/shard_map/bkij,bkjs->bis/dot_general | solution.py:40
  151.6 0.0 copy-done.3
  151.6 0.5 convolution_bitcast_fusion
  152.2 30.4 %psum.7 = f32[4,1024]{1,0:T(4,128)S(1)} all-reduce(f32[4,1024]{1,0:T(4,128)S(1)} %convolution_bitcast_fusion), channel_id=1, replica_groups=mesh['fix'=64,'subj'=8] {'subj'}, use_global_device_ids=true, to_apply=%region_2.3 | all-reduce | flops 4096 | bytes 32768 | tf_op jit(solution)/shard_map/psum | solution.py:44
  182.5 0.0 copy-done.4
  182.5 1.0 convolution_subtract_fusion
  183.5 3.2 %fusion.13 = f32[512,1024]{1,0:T(8,128)} fusion(f32[512,128]{1,0:T(8,128)S(1)} %bitcast.42, f32[1024,128]{1,0:T(8,128)S(1)} %convolution_subtract_fusion), kind=kOutput, calls=%fused_computation.49 | convolution fusion | flops 805306368 | bytes 2883584 | tf_op jit(solution)/shard_map/cs,fs->cf/dot_general | solution.py:46
  186.7 0.0 reduce-scatter.2.cloned.1.call-update
  186.7 38.6 %reduce-scatter.2.cloned.1.call-done = f32[64,1024]{1,0:T(8,128)} async-done(((f32[512,1024]{1,0:T(8,128)}), f32[64,1024]{1,0:T(8,128)}) %reduce-scatter.2.cloned.1.call-update) | async-done | bytes 262160 | tf_op jit(solution)/shard_map/reduce_scatter | solution.py:47
  (13 shorter events, 0.1 us)
Async XLA Ops:
  6.5 140.9 %copy-start = (f32[8,4,128,128]{3,2,1,0:T(8,128)S(1)}, f32[8,4,128,128]{3,2,1,0:T(8,128)}, u32[]{:S(2)}) copy-start(f32[8,4,128,128]{3,2,1,0:T(8,128)} %param.8) | copy-start | bytes 6291460
  39.7 7.5 %copy-start.2 = (f32[4,1024]{1,0:T(4,128)S(1)}, f32[4,1024]{1,0:T(4,128)}, u32[]{:S(2)}) copy-start(f32[4,1024]{1,0:T(4,128)} %param.12) | copy-start | bytes 49156
  39.7 7.7 %copy-start.1 = (s32[128,128]{1,0:T(8,128)S(1)}, s32[128,128]{1,0:T(8,128)}, u32[]{:S(2)}) copy-start(s32[128,128]{1,0:T(8,128)} %param.13) | copy-start | bytes 196612
  39.7 103.6 %all-to-all-start.1 = ((f32[64,1,128,128]{3,2,1,0:T(8,128)}), f32[64,1,128,128]{3,2,1,0:T(8,128)}, u32[]{:S(2)}, u32[]{:S(2)}) async-start(f32[64,1,128,128]{3,2,1,0:T(8,128)} %bitcast_select_fusion), calls=%async_computation.1 | async-start | bytes 8388608 | tf_op jit(solution)/shard_map/all_to_all | solution.py:36
  47.1 178.3 %reduce-scatter.2.cloned.1.call-start = ((), (), s32[]{:S(2)}) async-start(), calls=%async_computation.3 | async-start | bytes 2359296 | tf_op jit(solution)/shard_map/reduce_scatter | solution.py:47
  147.5 4.1 %copy-start.3 = (f32[4,128]{1,0:T(4,128)S(1)}, f32[4,128]{1,0:T(4,128)}, u32[]{:S(2)}) copy-start(f32[4,128]{1,0:T(4,128)} %param.11) | copy-start | bytes 6148
  147.5 35.1 %copy-start.4 = (f32[4,128]{1,0:T(4,128)S(1)}, f32[4,128]{1,0:T(4,128)}, u32[]{:S(2)}) copy-start(f32[4,128]{1,0:T(4,128)} %param.10) | copy-start | bytes 6148
Sparse Core Ops, SparseCore 0:
  186.8 38.4 reduce-scatter.1
where the time goes:
time: 233 us; the launch traced here: 232 us
  waiting for transfers between devices  74.4 us (32%)
  local copies, waits for them, and re-layouts  70.1 us (30%)
  blocking collectives  51.9 us (22%)
  between operations  13.5 us (6%)
  matrix products  8.82 us (4%)
  starting transfers between devices  7.41 us (3%)
  other arithmetic  6.09 us (3%)
    gather x2, local copies, waits for them, and re-layouts, design_rows(): picked = jnp.take(contrast, perm_table, axis=1)  59.9 us
    reduce_scatter x1, waiting for transfers between devices, per_device(): lax.psum_scatter(partial_value, 'subj', scatter_dimension=0, tiled=True)  38.6 us
    all_to_all x1, waiting for transfers between devices, per_device(): lax.all_to_all(outgoing, 'fix', split_axis=0, concat_axis=0, tiled=True)  35.7 us
    psum x1, blocking collectives, per_device(): fitted = lax.psum(fitted_part, 'subj')  30.4 us
    all_to_all x1, blocking collectives, per_device(): lax.all_to_all(request.reshape(fix_count, capacity), 'fix', split_axis=0,...  21.5 us
    all_to_all x1, starting transfers between devices, per_device(): lax.all_to_all(outgoing, 'fix', split_axis=0, concat_axis=0, tiled=True)  7.37 us
  transfers between devices with their start and end apart: 2, of which 2 were waited for; matrix products, arithmetic and copies ran while one was open for 26% of the time, Pallas kernels for 0%

commit v1 on v0

--- a/solution.py
+++ b/solution.py
@@ -2,6 +2,15 @@
 import jax.numpy as jnp
 from jax import lax
 from jax.sharding import PartitionSpec as P
+
+
+def added_up(x, name):
+    count = lax.axis_size(name)
+    total, reach = (x, 1)
+    while reach < count:
+        total = total + lax.ppermute(total, name, [(i, i ^ reach) for i in range(count)])
+        reach = 2 * reach
+    return total
 
 
 def design_rows(contrast, perm_table):
@@ -41,7 +50,7 @@
         "bkij,bkjs->bis", conn_tiles, needed, precision=lax.Precision.HIGHEST
     ).reshape(block_count * block_size, subj_count)
     fitted_part = jnp.einsum("ns,fs->nf", nuisance_pinv, smoothed, precision=lax.Precision.HIGHEST)
-    fitted = lax.psum(fitted_part, "subj")
+    fitted = added_up(fitted_part, "subj")
     residual = smoothed - jnp.einsum("nf,ns->fs", fitted, nuisance, precision=lax.Precision.HIGHEST)
     partial_value = jnp.einsum("cs,fs->cf", design, residual, precision=lax.Precision.HIGHEST)
     return lax.psum_scatter(partial_value, "subj", scatter_dimension=0, tiled=True)

time: 233 us -> 283 us (1.21)
  waiting for transfers between devices: 74.4 us -> 141 us
  blocking collectives: 51.9 us -> 21.5 us
  starting transfers between devices: 7.41 us -> 21.2 us
    all_to_all x1, waiting for transfers between devices: 35.7 us -> 96 us  [per_device(): lax.all_to_all(outgoing, 'fix', split_axis=0, concat_axis=0, tiled=True)]
    psum x1 -> x0, blocking collectives: 30.4 us -> none  [per_device(): fitted = lax.psum(fitted_part, 'subj')]
    ppermute x0 -> x3, starting transfers between devices: none -> 13.9 us  [added_up(): lax.ppermute(total, name, [(i, i ^ reach) for i in range(count)])]
    ppermute x0 -> x3, waiting for transfers between devices: none -> 5.6 us  [added_up(): lax.ppermute(total, name, [(i, i ^ reach) for i in range(count)])]
  transfers between devices with their start and end apart: 2 -> 5, of which waited for: 2 -> 4; matrix products, arithmetic and copies ran while one was open for 26% -> 21% of each run, Pallas kernels for 0% -> 0%
where the time goes in v1:
time: 283 us; the launch traced here: 282 us
  waiting for transfers between devices  141 us (50%)
  local copies, waits for them, and re-layouts  70.1 us (25%)
  blocking collectives  21.5 us (8%)
  starting transfers between devices  21.2 us (7%)
  between operations  13.6 us (5%)
  matrix products  8.81 us (3%)
  other arithmetic  6.12 us (2%)
    all_to_all x1, waiting for transfers between devices, per_device(): lax.all_to_all(outgoing, 'fix', split_axis=0, concat_axis=0, tiled=True)  96 us
    gather x2, local copies, waits for them, and re-layouts, design_rows(): picked = jnp.take(contrast, perm_table, axis=1)  59.9 us
    reduce_scatter x1, waiting for transfers between devices, per_device(): lax.psum_scatter(partial_value, 'subj', scatter_dimension=0, tiled=True)  39.3 us
    all_to_all x1, blocking collectives, per_device(): lax.all_to_all(request.reshape(fix_count, capacity), 'fix', split_axis=0,...  21.5 us
    ppermute x3, starting transfers between devices, added_up(): lax.ppermute(total, name, [(i, i ^ reach) for i in range(count)])  13.9 us
    all_to_all x1, starting transfers between devices, per_device(): lax.all_to_all(outgoing, 'fix', split_axis=0, concat_axis=0, tiled=True)  7.23 us
  transfers between devices with their start and end apart: 5, of which 4 were waited for; matrix products, arithmetic and copies ran while one was open for 21% of the time, Pallas kernels for 0%

profile of v1, /device:TPU:6, one launch (start us, length us, event | category | flops | bytes accessed | tf_op | source)
XLA Modules:
  0.0 282.2 jit_solution(9617141045570340068)
XLA Ops:
  6.5 0.9 copy.43
  7.4 0.1 reshape.202
  7.5 0.1 reshape.203
  7.6 0.2 convert_reduce_fusion
  7.8 0.7 scatter_custom_fusion
  8.5 0.1 copy.49
  8.6 21.5 %all_to_all.20 = s32[64,1,1]{2,1,0:T(1,128)S(1)} all-to-all(s32[64,1,1]{2,1,0:T(1,128)S(1)} %copy.49), channel_id=1, replica_groups=mesh['fix'=64,'subj'=8] {'fix'}, dimensions={0} | all-to-all | bytes 512 | tf_op jit(solution)/shard_map/all_to_all | solution.py:37
  30.1 1.2 reduce
  31.4 3.8 %gather_fusion.1 = f32[64,128,128]{2,1,0:T(8,128)} fusion(f32[8,128,128]{2,1,0:T(8,128)} %bitcast.36, s32[1024]{0:T(1024)S(1)} %pad_clamp_fusion.1), kind=kCustom, calls=%fused_computation.1 | custom fusion | bytes 8388864 | tf_op jit(solution)/shard_map/jit(_take)/gather | solution.py:42
  35.2 4.5 %bitcast_select_fusion = f32[64,1,128,128]{3,2,1,0:T(8,128)} fusion(f32[64,128,128]{2,1,0:T(8,128)} %gather_fusion.1, pred[64]{0:T(512)(128)(4,1)S(1)} %compare_and_fusion.2), kind=kLoop, calls=%fused_computation.4 | loop fusion | flops 1048576 | bytes 8388672 | tf_op jit(solution)/shard_map/jit(_take)/select_n | solution.py:42
  39.7 7.2 %all-to-all-start.1 = ((f32[64,1,128,128]{3,2,1,0:T(8,128)}), f32[64,1,128,128]{3,2,1,0:T(8,128)}, u32[]{:S(2)}, u32[]{:S(2)}) async-start(f32[64,1,128,128]{3,2,1,0:T(8,128)} %bitcast_select_fusion), calls=%async_computation.1 | async-start | bytes 8388608 | tf_op jit(solution)/shard_map/all_to_all | solution.py:45
  46.9 0.0 reduce-scatter.2.cloned.1.call-start
  47.0 0.1 reduce_sum.14
  47.1 96.0 %all-to-all-done.1 = f32[64,1,128,128]{3,2,1,0:T(8,128)} async-done(((f32[64,1,128,128]{3,2,1,0:T(8,128)}), f32[64,1,128,128]{3,2,1,0:T(8,128)}, u32[]{:S(2)}, u32[]{:S(2)}) %all-to-all-start.1) | async-done | bytes 4194336 | tf_op jit(solution)/shard_map/all_to_all | solution.py:45
  143.1 4.2 %gather_fusion.2 = f32[32,128,128]{2,1,0:T(8,128)} fusion(f32[64,128,128]{2,1,0:T(8,128)} %bitcast.10, s32[1024]{0:T(1024)S(1)} %pad_clamp_fusion), kind=kCustom, calls=%fused_computation.2 | custom fusion | bytes 4194432 | tf_op jit(solution)/shard_map/jit(_take)/gather | solution.py:48
  147.3 4.1 %fusion = f32[8,128,128,1]{1,2,3,0:T(8,128)S(1)} fusion(f32[8,4,128,128]{3,2,1,0:T(8,128)S(1)} %copy-done, f32[8,4,128,128]{3,2,1,0:T(8,128)} %bitcast.38, pred[8,4]{1,0:T(8,128)(4,1)S(1)} %compare_and_fusion.1), kind=kOutput, calls=%fused_computation.5 | convolution fusion | flops 805830656 | bytes 4718624 | tf_op jit(solution)/shard_map/bkij,bkjs->bis/dot_general | solution.py:49
  151.5 0.5 convolution_bitcast_fusion
  152.0 3.5 %collective-permute-start = (f32[4,1024]{1,0:T(4,128)S(1)}, f32[4,1024]{1,0:T(4,128)S(1)}, u32[]{:S(2)}, u32[]{:S(2)}) collective-permute-start(f32[4,1024]{1,0:T(4,128)S(1)} %convolution_bitcast_fusion), channel_id=1, source_target_pairs={{0,1},{1,0},{2,3},{3,2},{4,5},{5,4},{6,7},{7,6},{8,9},{9,8},{10,11... | collective-permute-start | bytes 49160 | tf_op jit(solution)/shard_map/ppermute | solution.py:11
  155.5 0.0 copy-done.1
  155.5 2.1 collective-permute-done
  157.7 4.5 %collective-permute-start.1 = (f32[4,1024]{1,0:T(4,128)S(1)}, f32[4,1024]{1,0:T(4,128)S(1)}, u32[]{:S(2)}, u32[]{:S(2)}) collective-permute-start(f32[4,1024]{1,0:T(4,128)S(1)} %add.116), channel_id=1, source_target_pairs={{0,2},{1,3},{2,0},{3,1},{4,6},{5,7},{6,4},{7,5},{8,10},{9,11},{10,... | collective-permute-start | bytes 49160 | tf_op jit(solution)/shard_map/ppermute | solution.py:11
  162.2 0.2 copy.41
  162.4 54.4 %gather_fusion = f32[16384,4]{1,0:T(8,128)} fusion(f32[4,1024]{0,1:T(8,128)S(1)} %copy.41, s32[16384]{0:T(1024)S(1)} %bitcast_clamp_fusion), kind=kCustom, calls=%fused_computation | custom fusion | bytes 589824 | tf_op jit(solution)/shard_map/jit(_take)/gather | solution.py:17
  216.8 5.5 %copy.42 = f32[128,128,4]{1,2,0:T(4,128)S(1)} copy(f32[128,128,4]{2,1,0:T(8,128)} %bitcast.37) | data formatting | bytes 524288 | tf_op jit(solution)/shard_map/jit(_take)/gather | solution.py:17
  222.3 0.0 collective-permute-done.1
  222.3 5.9 %collective-permute-start.2 = (f32[4,1024]{1,0:T(4,128)S(1)}, f32[4,1024]{1,0:T(4,128)S(1)}, u32[]{:S(2)}, u32[]{:S(2)}) collective-permute-start(f32[4,1024]{1,0:T(4,128)S(1)} %add.117), channel_id=1, source_target_pairs={{0,4},{1,5},{2,6},{3,7},{4,0},{5,1},{6,2},{7,3},{8,12},{9,13},{10,... | collective-permute-start | bytes 49160 | tf_op jit(solution)/shard_map/ppermute | solution.py:11
  228.3 0.1 broadcast_select_fusion
  228.4 3.5 %collective-permute-done.2 = f32[4,1024]{1,0:T(4,128)S(1)} collective-permute-done((f32[4,1024]{1,0:T(4,128)S(1)}, f32[4,1024]{1,0:T(4,128)S(1)}, u32[]{:S(2)}, u32[]{:S(2)}) %collective-permute-start.2) | collective-permute-done | bytes 16416 | tf_op jit(solution)/shard_map/ppermute | solution.py:11
  231.9 1.0 convolution_subtract_fusion
  232.9 3.1 %fusion.14 = f32[512,1024]{1,0:T(8,128)} fusion(f32[512,128]{1,0:T(8,128)S(1)} %bitcast.41, f32[1024,128]{1,0:T(8,128)S(1)} %convolution_subtract_fusion), kind=kOutput, calls=%fused_computation.50 | convolution fusion | flops 805306368 | bytes 2883584 | tf_op jit(solution)/shard_map/cs,fs->cf/dot_general | solution.py:55
  236.0 0.0 reduce-scatter.2.cloned.1.call-update
  236.1 39.3 %reduce-scatter.2.cloned.1.call-done = f32[64,1024]{1,0:T(8,128)} async-done(((f32[512,1024]{1,0:T(8,128)}), f32[64,1024]{1,0:T(8,128)}) %reduce-scatter.2.cloned.1.call-update) | async-done | bytes 262160 | tf_op jit(solution)/shard_map/reduce_scatter | solution.py:56
  (20 shorter events, 0.1 us)
Async XLA Ops:
  6.5 140.8 %copy-start = (f32[8,4,128,128]{3,2,1,0:T(8,128)S(1)}, f32[8,4,128,128]{3,2,1,0:T(8,128)}, u32[]{:S(2)}) copy-start(f32[8,4,128,128]{3,2,1,0:T(8,128)} %param.8) | copy-start | bytes 6291460
  39.7 103.4 %all-to-all-start.1 = ((f32[64,1,128,128]{3,2,1,0:T(8,128)}), f32[64,1,128,128]{3,2,1,0:T(8,128)}, u32[]{:S(2)}, u32[]{:S(2)}) async-start(f32[64,1,128,128]{3,2,1,0:T(8,128)} %bitcast_select_fusion), calls=%async_computation.1 | async-start | bytes 8388608 | tf_op jit(solution)/shard_map/all_to_all | solution.py:45
  46.9 228.5 %reduce-scatter.2.cloned.1.call-start = ((), (), s32[]{:S(2)}) async-start(), calls=%async_computation.3 | async-start | bytes 2359296 | tf_op jit(solution)/shard_map/reduce_scatter | solution.py:56
  147.3 4.1 %copy-start.3 = (f32[4,128]{1,0:T(4,128)S(1)}, f32[4,128]{1,0:T(4,128)}, u32[]{:S(2)}) copy-start(f32[4,128]{1,0:T(4,128)} %param.11) | copy-start | bytes 6148
  147.3 8.2 %copy-start.1 = (s32[128,128]{1,0:T(8,128)S(1)}, s32[128,128]{1,0:T(8,128)}, u32[]{:S(2)}) copy-start(s32[128,128]{1,0:T(8,128)} %param.13) | copy-start | bytes 196612
  147.3 14.9 %copy-start.2 = (f32[4,1024]{1,0:T(4,128)S(1)}, f32[4,1024]{1,0:T(4,128)}, u32[]{:S(2)}) copy-start(f32[4,1024]{1,0:T(4,128)} %param.12) | copy-start | bytes 49156
  152.0 5.6 %collective-permute-start = (f32[4,1024]{1,0:T(4,128)S(1)}, f32[4,1024]{1,0:T(4,128)S(1)}, u32[]{:S(2)}, u32[]{:S(2)}) collective-permute-start(f32[4,1024]{1,0:T(4,128)S(1)} %convolution_bitcast_fusion), channel_id=1, source_target_pairs={{0,1},{1,0},{2,3},{3,2},{4,5},{5,4},{6,7},{7,6},{8,9},{9,8},{10,11... | collective-permute-start | bytes 49160 | tf_op jit(solution)/shard_map/ppermute | solution.py:11
  157.7 64.7 %collective-permute-start.1 = (f32[4,1024]{1,0:T(4,128)S(1)}, f32[4,1024]{1,0:T(4,128)S(1)}, u32[]{:S(2)}, u32[]{:S(2)}) collective-permute-start(f32[4,1024]{1,0:T(4,128)S(1)} %add.116), channel_id=1, source_target_pairs={{0,2},{1,3},{2,0},{3,1},{4,6},{5,7},{6,4},{7,5},{8,10},{9,11},{10,... | collective-permute-start | bytes 49160 | tf_op jit(solution)/shard_map/ppermute | solution.py:11
  216.8 15.1 %copy-start.4 = (f32[4,128]{1,0:T(4,128)S(1)}, f32[4,128]{1,0:T(4,128)}, u32[]{:S(2)}) copy-start(f32[4,128]{1,0:T(4,128)} %param.10) | copy-start | bytes 6148
  222.3 9.5 %collective-permute-start.2 = (f32[4,1024]{1,0:T(4,128)S(1)}, f32[4,1024]{1,0:T(4,128)S(1)}, u32[]{:S(2)}, u32[]{:S(2)}) collective-permute-start(f32[4,1024]{1,0:T(4,128)S(1)} %add.117), channel_id=1, source_target_pairs={{0,4},{1,5},{2,6},{3,7},{4,0},{5,1},{6,2},{7,3},{8,12},{9,13},{10,... | collective-permute-start | bytes 49160 | tf_op jit(solution)/shard_map/ppermute | solution.py:11
Sparse Core Ops, SparseCore 0:
  236.2 39.1 reduce-scatter.1
